TPU v7x, 32 devices: a whole 2x2x4 slice. The times are simulated.
32 devices in a mesh: batch: 4 (over y, x), ctx: 8 (over z, core).
Axes of the slice: x: 2, y: 2, z: 4, core: 2. Of those that a mesh axis runs over, the one named last changes fastest.
Arguments:
- hidden: bfloat16 [4, 1024, 768], P('batch', 'ctx'), may hold values from -6 to 6
- cotangent: bfloat16 [4, 1024, 768], P('batch', 'ctx'), may hold values from -6 to 6
- w_qkv: bfloat16 [768, 2304], P(('batch', 'ctx')), may hold values from -3 to 3
- w_proj: bfloat16 [768, 768], P(('batch', 'ctx')), may hold values from -1.25 to 1.25
- w_inner: bfloat16 [768, 2304], P(('batch', 'ctx')), may hold values from -0.21875 to 0.21875
- w_down: bfloat16 [768, 1152], P(('batch', 'ctx')), may hold values from -0.1875 to 0.1875
- norm1_gain: bfloat16 [768], P(('batch', 'ctx')), may hold values from 0.5 to 1.5
- norm2_gain: bfloat16 [768], P(('batch', 'ctx')), may hold values from 0.5 to 1.5
Outputs:
- hidden_out: bfloat16 [4, 1024, 768], P('batch', 'ctx')
- hidden_grad: float32 [4, 1024, 768], P('batch', 'ctx')
- qkv_grad: float32 [768, 2304], P(('batch', 'ctx'))
- proj_grad: float32 [768, 768], P(('batch', 'ctx'))
- inner_grad: float32 [768, 2304], P(('batch', 'ctx'))
- down_grad: float32 [768, 1152], P(('batch', 'ctx'))
- norm1_grad: float32 [768], P(('batch', 'ctx'))
- norm2_grad: float32 [768], P(('batch', 'ctx'))
All inputs are finite; a program needn't handle non-finite values.
Results may differ from a plain program's by a relative error of at most 0.02.
Values may be sent and summed in bfloat16 or wider, within the bound.
A program may use at most 192 MiB of HBM per device.

v0:
```python
import jax
import jax.numpy as jnp
from jax import lax
from jax.sharding import PartitionSpec as P

D = 768
HEADS = 12
HEAD_DIM = 64
FF = 1152
norm_eps = 1e-05
rope_base = 160000.0


def apply_layer_norm(values, gain_vector):
    centre = jnp.mean(values, axis=-1, keepdims=True)
    shifted = values - centre
    spread = jnp.mean(shifted * shifted, axis=-1, keepdims=True)
    inverse = lax.rsqrt(spread + norm_eps)
    normed = shifted * inverse
    return (normed * gain_vector, normed, inverse)


def layer_norm_gradient(upstream, gain_vector, normed, inverse):
    scaled = upstream * gain_vector
    first_mean = jnp.mean(scaled, axis=-1, keepdims=True)
    second_mean = jnp.mean(scaled * normed, axis=-1, keepdims=True)
    return (
        inverse * (scaled - first_mean - normed * second_mean),
        jnp.sum(upstream * normed, axis=0),
    )


def rope_tables(offset, row_count, head_width):
    half_dim = head_width // 2
    position = (offset + jnp.arange(row_count, dtype=jnp.int32)).astype(jnp.float32)
    exponent = jnp.arange(half_dim, dtype=jnp.int32).astype(jnp.float32) * (-2.0 / head_width)
    angles = position[:, None] * jnp.power(rope_base, exponent)[None, :]
    return (jnp.cos(angles), jnp.sin(angles))


def rotate(values, cosine, sine_table, direction):
    half_dim = values.shape[-1] // 2
    front_half = values[..., :half_dim]
    back_half = values[..., half_dim:]
    cos_rows = cosine[:, None, :]
    sin_rows = sine_table[:, None, :] * direction
    return jnp.concatenate(
        [
            front_half * cos_rows - back_half * sin_rows,
            back_half * cos_rows + front_half * sin_rows,
        ],
        axis=-1,
    )


def gelu_parts(act_input):
    normal_cdf = 0.5 * (1.0 + jax.scipy.special.erf(act_input * 0.7071067811865476))
    density = jnp.exp(-0.5 * act_input * act_input) * 0.3989422804014327
    return (act_input * normal_cdf, normal_cdf + act_input * density)


def as_heads(flat_rows):
    return flat_rows.reshape(flat_rows.shape[0], HEADS, HEAD_DIM)


def pair_terms(query_rows, grad_rows, log_rows, delta_rows, key_rows, value_rows, score_scale):
    scores = (
        jnp.einsum("qhd,khd->hqk", query_rows, key_rows, preferred_element_type=jnp.float32)
        * score_scale
    )
    probabilities = jnp.exp(scores - log_rows[..., None])
    grad_dots = jnp.einsum(
        "qhd,khd->hqk", grad_rows, value_rows, preferred_element_type=jnp.float32
    )
    dscore = (probabilities * (grad_dots - delta_rows[..., None])).astype(jnp.bfloat16)
    return (probabilities.astype(jnp.bfloat16), dscore)


def local(hidden, cotangent, w_qkv, w_proj, w_inner, w_down, norm1_gain, norm2_gain):
    token_rows = hidden.shape[1]
    score_scale = HEAD_DIM ** (-0.5)
    full_qkv, full_proj, full_inner, full_down, gain_first, gain_second = (
        lax.all_gather(w_qkv, ("batch", "ctx"), axis=0, tiled=True),
        lax.all_gather(w_proj, ("batch", "ctx"), axis=0, tiled=True),
        lax.all_gather(w_inner, ("batch", "ctx"), axis=0, tiled=True),
        lax.all_gather(w_down, ("batch", "ctx"), axis=0, tiled=True),
        lax.all_gather(norm1_gain, ("batch", "ctx"), axis=0, tiled=True),
        lax.all_gather(norm2_gain, ("batch", "ctx"), axis=0, tiled=True),
    )
    first_norm_gain = gain_first.astype(jnp.float32)
    second_norm_gain = gain_second.astype(jnp.float32)
    input_tokens = hidden[0].astype(jnp.float32)
    first_normed_rows, first_centered_rows, first_inverse_deviation = apply_layer_norm(
        input_tokens, first_norm_gain
    )
    h_one = first_normed_rows.astype(jnp.bfloat16)
    projected = jnp.dot(h_one, full_qkv, preferred_element_type=jnp.float32)
    cosine, sine_table = rope_tables(lax.axis_index("ctx") * token_rows, token_rows, HEAD_DIM)
    query_rot = rotate(as_heads(projected[:, :D]), cosine, sine_table, 1.0).astype(jnp.bfloat16)
    key_flat = (
        rotate(as_heads(projected[:, D : 2 * D]), cosine, sine_table, 1.0)
        .astype(jnp.bfloat16)
        .reshape(token_rows, D)
    )
    value_flat = projected[:, 2 * D :].astype(jnp.bfloat16)
    key_rot = as_heads(key_flat)
    value_rows = as_heads(value_flat)
    zero_heads = jnp.zeros((token_rows, HEADS, HEAD_DIM), jnp.float32)
    piece_rows = (
        lax.all_gather(key_flat, "ctx", axis=0, tiled=True),
        lax.all_gather(value_flat, "ctx", axis=0, tiled=True),
    )
    row_peak = jnp.full((HEADS, token_rows), -jnp.inf, jnp.float32)
    row_total = jnp.zeros((HEADS, token_rows), jnp.float32)
    key_piece = as_heads(piece_rows[0])
    value_piece = as_heads(piece_rows[1])
    scores = (
        jnp.einsum("qhd,khd->hqk", query_rot, key_piece, preferred_element_type=jnp.float32)
        * score_scale
    )
    new_peak = jnp.max(scores, axis=-1)
    row_fade = jnp.exp(row_peak - new_peak)
    probabilities = jnp.exp(scores - new_peak[..., None])
    new_total = row_total * row_fade + jnp.sum(probabilities, axis=-1)
    new_mixture = zero_heads * jnp.transpose(row_fade)[:, :, None] + jnp.einsum(
        "hqk,khd->qhd",
        probabilities.astype(jnp.bfloat16),
        value_piece,
        preferred_element_type=jnp.float32,
    )
    log_total = new_peak + jnp.log(new_total)
    attended = (
        (new_mixture / jnp.transpose(new_total)[:, :, None])
        .reshape(token_rows, D)
        .astype(jnp.bfloat16)
    )
    residual_stream = input_tokens + jnp.dot(
        attended, full_proj, preferred_element_type=jnp.float32
    )
    second_normed_rows, second_centered_rows, second_inverse_deviation = apply_layer_norm(
        residual_stream, second_norm_gain
    )
    h_two = second_normed_rows.astype(jnp.bfloat16)
    inner_all = jnp.dot(h_two, full_inner, preferred_element_type=jnp.float32)
    act_half = inner_all[:, :FF]
    gate_half = inner_all[:, FF:]
    activated, gelu_slope = gelu_parts(act_half)
    middle = (activated * gate_half).astype(jnp.bfloat16)
    output_rows = residual_stream + jnp.einsum(
        "tf,df->td", middle, full_down, preferred_element_type=jnp.float32
    )
    back_qkv, back_proj, back_inner, back_down = (full_qkv, full_proj, full_inner, full_down)
    upstream = cotangent[0]
    d_middle = jnp.dot(upstream, back_down, preferred_element_type=jnp.float32)
    d_inner = jnp.concatenate(
        [d_middle * gate_half * gelu_slope, d_middle * activated], axis=-1
    ).astype(jnp.bfloat16)
    second_hidden_gradient = jnp.einsum(
        "te,de->td", d_inner, back_inner, preferred_element_type=jnp.float32
    )
    residual_norm_gradient, second_gain_portion = layer_norm_gradient(
        second_hidden_gradient, second_norm_gain, second_centered_rows, second_inverse_deviation
    )
    d_resid = upstream.astype(jnp.float32) + residual_norm_gradient
    d_resid_low = d_resid.astype(jnp.bfloat16)
    d_attended = jnp.einsum(
        "td,ed->te", d_resid_low, back_proj, preferred_element_type=jnp.float32
    ).astype(jnp.bfloat16)
    grad_heads = as_heads(d_attended)
    row_delta = jnp.transpose(
        jnp.sum(grad_heads.astype(jnp.float32) * as_heads(attended).astype(jnp.float32), axis=-1)
    )
    log_whole, delta_whole = (
        lax.all_gather(log_total, "ctx", axis=1, tiled=True),
        lax.all_gather(row_delta, "ctx", axis=1, tiled=True),
    )
    piece_rows = (
        lax.all_gather(key_flat, "ctx", axis=0, tiled=True),
        lax.all_gather(value_flat, "ctx", axis=0, tiled=True),
    )
    key_part = as_heads(piece_rows[0])
    value_part = as_heads(piece_rows[1])
    probs_low, dscore = pair_terms(
        query_rot, grad_heads, log_total, row_delta, key_part, value_part, score_scale
    )
    query_grad = (
        jnp.einsum("hqk,khd->qhd", dscore, key_part, preferred_element_type=jnp.float32)
        * score_scale
    )
    piece_rows = (
        lax.all_gather(query_rot.reshape(token_rows, D), "ctx", axis=0, tiled=True),
        lax.all_gather(d_attended, "ctx", axis=0, tiled=True),
    )
    query_part = as_heads(piece_rows[0])
    grad_part = as_heads(piece_rows[1])
    probs_low, dscore = pair_terms(
        query_part, grad_part, log_whole, delta_whole, key_rot, value_rows, score_scale
    )
    key_sum = (
        jnp.einsum("hqk,qhd->khd", dscore, query_part, preferred_element_type=jnp.float32)
        * score_scale
    )
    value_sum = jnp.einsum("hqk,qhd->khd", probs_low, grad_part, preferred_element_type=jnp.float32)
    d_query = rotate(query_grad, cosine, sine_table, -1.0)
    d_key = rotate(key_sum, cosine, sine_table, -1.0)
    d_projected = jnp.concatenate(
        [
            d_query.reshape(token_rows, D),
            d_key.reshape(token_rows, D),
            value_sum.reshape(token_rows, D),
        ],
        axis=-1,
    ).astype(jnp.bfloat16)
    first_hidden_gradient = jnp.einsum(
        "te,de->td", d_projected, back_qkv, preferred_element_type=jnp.float32
    )
    input_norm_gradient, first_gain_portion = layer_norm_gradient(
        first_hidden_gradient, first_norm_gain, first_centered_rows, first_inverse_deviation
    )
    input_grad = d_resid + input_norm_gradient

    def grad_rows(start, count):
        return jnp.concatenate(
            [
                jnp.einsum("td,te->de", h_one, d_projected, preferred_element_type=jnp.float32),
                jnp.einsum("te,td->ed", attended, d_resid_low, preferred_element_type=jnp.float32),
                jnp.einsum("td,te->de", h_two, d_inner, preferred_element_type=jnp.float32),
                jnp.einsum("td,tf->df", upstream, middle, preferred_element_type=jnp.float32),
                first_gain_portion[:, None],
                second_gain_portion[:, None],
            ],
            axis=1,
        )

    owned_rows = D // lax.axis_size(("batch", "ctx"))
    grad_share = lax.psum_scatter(
        grad_rows(jnp.int32(0), owned_rows * lax.axis_size(("batch", "ctx"))),
        ("batch", "ctx"),
        scatter_dimension=0,
        tiled=True,
    )
    qkv_share = grad_share[:, : 3 * D]
    proj_share = grad_share[:, 3 * D : 4 * D]
    inner_share = grad_share[:, 4 * D : 4 * D + 2 * FF]
    down_share = grad_share[:, 4 * D + 2 * FF : 4 * D + 3 * FF]
    first_share = grad_share[:, 4 * D + 3 * FF]
    second_share = grad_share[:, 4 * D + 3 * FF + 1]
    return (
        output_rows.astype(jnp.bfloat16)[None],
        input_grad[None],
        qkv_share,
        proj_share,
        inner_share,
        down_share,
        first_share,
        second_share,
    )


def solution(mesh):
    placed = (
        P("batch", "ctx", None),
        P("batch", "ctx", None),
        P(("batch", "ctx"), None),
        P(("batch", "ctx"), None),
        P(("batch", "ctx"), None),
        P(("batch", "ctx"), None),
        P(("batch", "ctx")),
        P(("batch", "ctx")),
    )
    return jax.shard_map(
        local,
        mesh=mesh,
        in_specs=placed,
        out_specs=(
            P("batch", "ctx", None),
            P("batch", "ctx", None),
            P(("batch", "ctx"), None),
            P(("batch", "ctx"), None),
            P(("batch", "ctx"), None),
            P(("batch", "ctx"), None),
            P(("batch", "ctx")),
            P(("batch", "ctx")),
        ),
        check_vma=False,
    )
```

profile of v0, /device:TPU:0, one launch (start us, length us, event | category | flops | bytes accessed | tf_op | source)
XLA Modules:
  0.0 641.2 jit_solution(14519602445404281982)
XLA Ops:
  8.0 0.8 dynamic-update-slice
  8.8 0.8 dynamic-update-slice.1
  9.6 42.2 %all-reduce.2 = (bf16[768]{0:T(1024)(128)(2,1)S(1)}, bf16[768]{0:T(1024)(128)(2,1)S(1)}) all-reduce(bf16[768]{0:T(1024)(128)(2,1)S(1)} %dynamic-update-slice, bf16[768]{0:T(1024)(128)(2,1)S(1)} %dynamic-update-slice.1), channel_id=1, replica_groups=mesh['batch'=4,'ctx'=8] {'batch','ctx'}, use_global_device_ids=true, to_apply=%add | all-reduce | flops 1536 | bytes 6144
  51.9 1.0 convert_reduce_fusion
  52.9 1.1 fusion.58
  54.1 0.8 broadcast_multiply_fusion
  54.8 19.1 %all-gather.9.cloned.1.call-done = bf16[768,2304]{1,0:T(8,128)(2,1)} async-done(((bf16[24,2304]{1,0:T(8,128)(2,1)}), bf16[768,2304]{1,0:T(8,128)(2,1)}) %all-gather.9.cloned.1.call-update) | async-done | bytes 3538960 | tf_op jit(solution)/shard_map/all_gather | solution.py:83
  73.9 2.8 fusion.79
  82.0 22.7 %all-gather.11.cloned.1.call-done = bf16[1024,768]{0,1:T(8,128)(2,1)} async-done(((bf16[128,768]{0,1:T(8,128)(2,1)}), bf16[1024,768]{0,1:T(8,128)(2,1)}) %all-gather.11.cloned.1.call-update) | async-done | bytes 1572880 | tf_op jit(solution)/shard_map/all_gather | solution.py:110
  104.7 2.5 multiply_reduce_fusion
  107.2 1.3 fusion
  108.5 1.4 copy-done
  109.9 21.1 %all-gather.13.cloned.1.call-done = bf16[1024,768]{1,0:T(8,128)(2,1)} async-done(((bf16[128,768]{1,0:T(8,128)(2,1)}), bf16[1024,768]{1,0:T(8,128)(2,1)}) %all-gather.13.cloned.1.call-update) | async-done | bytes 1572880 | tf_op jit(solution)/shard_map/all_gather | solution.py:111
  131.0 1.7 copy.27
  132.7 4.8 fusion.35
  137.5 49.6 %all-gather.15.cloned.1.call-done = bf16[768,768]{1,0:T(8,128)(2,1)} async-done(((bf16[24,768]{1,0:T(8,128)(2,1)}), bf16[768,768]{1,0:T(8,128)(2,1)}) %all-gather.15.cloned.1.call-update) | async-done | bytes 1179664 | tf_op jit(solution)/shard_map/all_gather | solution.py:84
  187.1 1.7 fusion.84
  189.1 59.9 %all-gather.17.cloned.1.call-done = bf16[768,2304]{1,0:T(8,128)(2,1)} async-done(((bf16[24,2304]{1,0:T(8,128)(2,1)}), bf16[768,2304]{1,0:T(8,128)(2,1)}) %all-gather.17.cloned.1.call-update) | async-done | bytes 3538960 | tf_op jit(solution)/shard_map/all_gather | solution.py:85
  249.0 2.7 fusion.81
  251.6 54.4 %all-gather.19.cloned.1.call-done = bf16[768,1152]{1,0:T(8,128)(2,1)} async-done(((bf16[24,1152]{1,0:T(8,128)(2,1)}), bf16[768,1152]{1,0:T(8,128)(2,1)}) %all-gather.19.cloned.1.call-update) | async-done | bytes 1769488 | tf_op jit(solution)/shard_map/all_gather | solution.py:86
  306.1 2.2 fusion.43
  308.6 1.4 multiply_reduce_fusion.1
  310.3 1.2 convolution_convert_fusion
  311.6 0.8 copy.30
  312.4 1.1 copy.28
  313.5 0.9 broadcast_in_dim.19
  314.4 15.1 %all_gather.47 = f32[12,1024]{1,0:T(8,128)} all-gather(f32[12,128]{1,0:T(8,128)S(1)} %get-tuple-element.36), channel_id=1, replica_groups=mesh['batch'=4,'ctx'=8] {'ctx'}, dimensions={1}, use_global_device_ids=true | all-gather | bytes 55296 | tf_op jit(solution)/shard_map/all_gather | solution.py:174
  329.6 15.2 %all_gather.49 = f32[12,1024]{1,0:T(8,128)} all-gather(f32[12,128]{1,0:T(8,128)S(1)} %bitcast.128), channel_id=1, replica_groups=mesh['batch'=4,'ctx'=8] {'ctx'}, dimensions={1}, use_global_device_ids=true | all-gather | bytes 55296 | tf_op jit(solution)/shard_map/all_gather | solution.py:175
  345.3 3.8 convolution_bitcast_fusion
  349.1 4.1 fusion.59
  353.2 5.1 fusion.85
  358.4 7.3 %fusion.23 = f32[128,12,64]{0,2,1:T(8,128)} fusion(bf16[1024,12,64]{0,2,1:T(8,128)(2,1)} %bitcast.114, f32[12,128,1024]{2,1,0:T(8,128)} %copy-done, f32[12,128]{1,0:T(8,128)S(1)} %bitcast.129, f32[12,128]{1,0:T(8,128)} %copy-done.21, bf16[128,12,64]{0,2,1:T(8,128)(2,1)} %bitcast.120, bf16[1024,12,64]{0,2,1:T(8,128)(2,1)} %bitcast.110), kind=kOutput, calls=%fused_computation.25 | convolution fusion | flops 410615808 | bytes 10039296 | tf_op jit(solution)/shard_map/hqk,khd->qhd/dot_general | solution.py:187
  365.6 2.6 copy.29
  368.2 4.5 fusion.28
  372.7 8.9 %fusion.21 = f32[128,12,64]{0,2,1:T(8,128)} fusion(bf16[1024,12,64]{0,2,1:T(8,128)(2,1)} %bitcast.116, f32[12,1024,128]{2,1,0:T(8,128)} %fusion.85, f32[12,1024]{1,0:T(8,128)} %all_gather.49, f32[12,1024]{1,0:T(8,128)} %all_gather.47, bf16[1024,12,64]{0,2,1:T(8,128)(2,1)} %bitcast.106, bf16[128,12,64]{0,2,1:T(8,128)(2,1)} %bitcast.127), kind=kOutput, calls=%fused_computation.23 | convolution fusion | flops 410615808 | bytes 10125312 | tf_op jit(solution)/shard_map/hqk,qhd->khd/dot_general | solution.py:200
  381.6 1.4 subtract_convert_fusion.1
  383.0 4.1 fusion.61
  387.1 2.6 fusion.57
  389.7 0.9 broadcast_in_dim.18
  390.6 22.2 %concatenate.31 = f32[768,6530]{1,0:T(8,128)} concatenate(f32[768,2304]{1,0:T(8,128)} %fusion.61, f32[768,768]{1,0:T(8,128)S(1)} %fusion.66, f32[768,2304]{1,0:T(8,128)} %fusion.59, f32[768,1152]{1,0:T(8,128)} %convolution_bitcast_fusion, f32[768,1]{1,0:T(8,128)} %broadcast_in_dim.18, f32[768,1]{1,0:T(8,128)} %broadcast_in_dim.19), dimensions={1} | concatenate | bytes 40120320 | tf_op jit(solution)/shard_map/concatenate | solution.py:223
  412.9 1.2 copy-done.4
  414.1 2.9 fusion.31
  417.0 0.9 fusion.56
  417.9 210.3 %reduce-scatter.2.cloned.1.call-done = f32[24,6530]{1,0:T(8,128)} async-done(((f32[768,6530]{1,0:T(8,128)}), f32[24,6530]{1,0:T(8,128)}) %reduce-scatter.2.cloned.1.call-update) | async-done | bytes 626896 | tf_op jit(solution)/shard_map/reduce_scatter | solution.py:236
  628.3 1.5 slice_reduce_fusion
  629.7 1.5 slice.91
  631.3 1.5 slice.93
  632.8 1.8 fusion.83
  (108 shorter events, 7.3 us)
Async XLA Ops:
  7.2 66.8 %all-gather.9.cloned.1.call-start = ((), (), s32[]{:S(2)}) async-start(), calls=%async_computation.1 | async-start | bytes 3649536 | tf_op jit(solution)/shard_map/all_gather | solution.py:83
  7.9 96.8 %all-gather.11.cloned.1.call-start = ((), (), s32[]{:S(2)}) async-start(), calls=%async_computation.2 | async-start | bytes 1769472 | tf_op jit(solution)/shard_map/all_gather | solution.py:110
  52.9 23.9 %copy-start.22 = (f32[128]{0:T(128)}, f32[128]{0:T(128)S(1)}, u32[]{:S(2)}) copy-start(f32[128]{0:T(128)S(1)} %broadcast_multiply_fusion.6) | copy-start | bytes 1540
  54.1 22.7 %copy-start.26 = (f32[128]{0:T(128)}, f32[128]{0:T(128)S(1)}, u32[]{:S(2)}) copy-start(f32[128]{0:T(128)S(1)} %add_rsqrt_fusion.1) | copy-start | bytes 1540
  54.8 22.3 %copy-start.20 = (f32[128,32]{0,1:T(8,128)}, f32[128,32]{0,1:T(8,128)S(1)}, u32[]{:S(2)}) copy-start(f32[128,32]{0,1:T(8,128)S(1)} %get-tuple-element.40) | copy-start | bytes 49156
  77.3 0.6 copy-start.9
  77.3 1.3 copy-start.11
  78.6 52.3 %all-gather.13.cloned.1.call-start = ((), (), s32[]{:S(2)}) async-start(), calls=%async_computation.3 | async-start | bytes 1769472 | tf_op jit(solution)/shard_map/all_gather | solution.py:111
  79.4 107.7 %all-gather.15.cloned.1.call-start = ((), (), s32[]{:S(2)}) async-start(), calls=%async_computation.4 | async-start | bytes 1216512 | tf_op jit(solution)/shard_map/all_gather | solution.py:84
  80.0 169.0 %all-gather.17.cloned.1.call-start = ((), (), s32[]{:S(2)}) async-start(), calls=%async_computation.5 | async-start | bytes 3649536 | tf_op jit(solution)/shard_map/all_gather | solution.py:85
  80.6 225.5 %all-gather.19.cloned.1.call-start = ((), (), s32[]{:S(2)}) async-start(), calls=%async_computation.6 | async-start | bytes 1824768 | tf_op jit(solution)/shard_map/all_gather | solution.py:86
  81.2 272.1 %all-gather.21.cloned.1.call-start = ((), (), s32[]{:S(2)}) async-start(), calls=%async_computation.7 | async-start | bytes 1769472 | tf_op jit(solution)/shard_map/all_gather | solution.py:191
  81.9 283.7 %all-gather.23.cloned.1.call-start = ((), (), s32[]{:S(2)}) async-start(), calls=%async_computation.8 | async-start | bytes 1769472 | tf_op jit(solution)/shard_map/all_gather | solution.py:192
  107.2 2.7 copy-start
  109.9 204.6 %copy-start.21 = (f32[12,128]{1,0:T(8,128)}, f32[12,128]{1,0:T(8,128)S(1)}, u32[]{:S(2)}) copy-start(f32[12,128]{1,0:T(8,128)S(1)} %get-tuple-element.36) | copy-start | bytes 18436
  132.7 4.8 copy-start.8
  132.7 54.4 %copy-start.1 = (bf16[1,128,768]{2,1,0:T(8,128)(2,1)S(1)}, bf16[1,128,768]{2,1,0:T(8,128)(2,1)}, u32[]{:S(2)}) copy-start(bf16[1,128,768]{2,1,0:T(8,128)(2,1)} %param.8) | copy-start | bytes 589828
  188.9 117.2 %copy-start.13 = (bf16[1,128,768]{2,1,0:T(8,128)(2,1)S(1)}, bf16[1,128,768]{2,1,0:T(8,128)(2,1)}, u32[]{:S(2)}) copy-start(bf16[1,128,768]{2,1,0:T(8,128)(2,1)} %param.9) | copy-start | bytes 589828
  188.9 121.2 %copy-start.24 = (f32[128]{0:T(128)}, f32[128]{0:T(128)S(1)}, u32[]{:S(2)}) copy-start(f32[128]{0:T(128)S(1)} %broadcast_multiply_fusion.5) | copy-start | bytes 1540
  189.1 121.0 %copy-start.28 = (f32[128]{0:T(128)}, f32[128]{0:T(128)S(1)}, u32[]{:S(2)}) copy-start(f32[128]{0:T(128)S(1)} %add_rsqrt_fusion) | copy-start | bytes 1540
  251.6 56.7 %copy-start.3 = (f32[128,2304]{1,0:T(8,128)}, f32[128,2304]{1,0:T(8,128)S(1)}, u32[]{:S(2)}) copy-start(f32[128,2304]{1,0:T(8,128)S(1)} %fusion.81) | copy-start | bytes 3538948
  306.1 2.5 copy-start.5
  308.3 1.7 copy-start.18
  308.3 2.0 copy-start.16
  308.6 1.7 copy-start.2
  308.6 3.0 copy-start.7
  311.5 316.7 %reduce-scatter.2.cloned.1.call-start = ((), (), s32[]{:S(2)}) async-start(), calls=%async_computation.9 | async-start | bytes 21086208 | tf_op jit(solution)/shard_map/reduce_scatter | solution.py:236
  313.5 16.1 %copy-start.14 = (bf16[128,768]{0,1:T(8,128)(2,1)}, bf16[128,768]{0,1:T(8,128)(2,1)S(1)}, u32[]{:S(2)}) copy-start(bf16[128,768]{0,1:T(8,128)(2,1)S(1)} %copy.28) | copy-start | bytes 589828
  344.8 4.2 copy-start.17
  344.8 4.2 copy-start.19
  344.8 4.2 copy-start.25
  344.8 4.2 copy-start.29
  349.1 4.2 copy-start.10
  349.1 4.1 copy-start.12
  372.7 10.3 %copy-start.23 = (f32[128]{0:T(128)S(1)}, f32[128]{0:T(128)}, u32[]{:S(2)}) copy-start(f32[128]{0:T(128)} %copy-done.22) | copy-start | bytes 1540
  372.7 10.3 %copy-start.27 = (f32[128]{0:T(128)S(1)}, f32[128]{0:T(128)}, u32[]{:S(2)}) copy-start(f32[128]{0:T(128)} %copy-done.26) | copy-start | bytes 1540
  383.0 4.1 copy-start.6
  412.8 1.3 copy-start.4
  412.8 4.2 copy-start.30
  414.1 2.9 copy-start.15
Sparse Core Ops, SparseCore 0:
  11.0 62.9 all-gather.8
  78.8 25.8 all-gather.10
  106.9 24.0 all-gather.12
  133.9 53.2 all-gather.14
  190.0 58.9 all-gather.16
  251.7 54.3 all-gather.18
  308.2 26.2 all-gather.20
  336.8 24.9 all-gather.22
  413.0 215.2 reduce-scatter.1
where the time goes:
time: 642 us; the launch traced here: 641 us
  waiting for transfers between devices  439 us (68%)
  blocking collectives  72.5 us (11%)
  matrix products  62.9 us (10%)
  local copies, waits for them, and re-layouts  43 us (7%)
  between operations  14.3 us (2%)
  other arithmetic  8.55 us (1%)
    reduce_scatter x1, waiting for transfers between devices, local(): lax.psum_scatter(grad_rows(jnp.int32(0), owned_rows * lax.axis_size(('bat...  210 us
    all_gather x1, waiting for transfers between devices, local(): lax.all_gather(w_inner, ('batch', 'ctx'), axis=0, tiled=True)  59.9 us
    all_gather x1, waiting for transfers between devices, local(): lax.all_gather(w_down, ('batch', 'ctx'), axis=0, tiled=True)  54.4 us
    all_gather x1, waiting for transfers between devices, local(): lax.all_gather(w_proj, ('batch', 'ctx'), axis=0, tiled=True)  49.6 us
    unnamed x1, blocking collectives  42.2 us
    all_gather x1, waiting for transfers between devices, local(): lax.all_gather(key_flat, 'ctx', axis=0, tiled=True)  22.7 us
    concatenate x1, local copies, waits for them, and re-layouts, grad_rows(): jnp.concatenate([jnp.einsum('td,te->de', h_one, d_projected, preferred_el...  22.2 us
    all_gather x1, waiting for transfers between devices, local(): lax.all_gather(value_flat, 'ctx', axis=0, tiled=True)  21.1 us
  transfers between devices with their start and end apart: 9, of which 7 were waited for; matrix products, arithmetic and copies ran while one was open for 8% of the time, Pallas kernels for 0%

commit v1 on v0

--- a/solution.py
+++ b/solution.py
@@ -77,12 +77,24 @@
 
 
 def local(hidden, cotangent, w_qkv, w_proj, w_inner, w_down, norm1_gain, norm2_gain):
+
+    def touch_shifts_all(here_x):
+        axis_len = lax.psum(1, axis_name=("batch", "ctx"))
+        s_next = range(here_x.ndim)
+        out_arr = map(lambda q: axis_len if q == 0 else 1, s_next)
+        x_now = list(out_arr)
+        current_value = jnp.tile(here_x, x_now)
+        a_now = lax.all_to_all(
+            current_value, axis_name=("batch", "ctx"), split_axis=0, concat_axis=0, tiled=True
+        )
+        return a_now
+
     token_rows = hidden.shape[1]
     score_scale = HEAD_DIM ** (-0.5)
     full_qkv, full_proj, full_inner, full_down, gain_first, gain_second = (
         lax.all_gather(w_qkv, ("batch", "ctx"), axis=0, tiled=True),
         lax.all_gather(w_proj, ("batch", "ctx"), axis=0, tiled=True),
-        lax.all_gather(w_inner, ("batch", "ctx"), axis=0, tiled=True),
+        touch_shifts_all(w_inner),
         lax.all_gather(w_down, ("batch", "ctx"), axis=0, tiled=True),
         lax.all_gather(norm1_gain, ("batch", "ctx"), axis=0, tiled=True),
         lax.all_gather(norm2_gain, ("batch", "ctx"), axis=0, tiled=True),

time: 642 us -> 619 us (0.964)
  waiting for transfers between devices: 439 us -> 411 us
    all_gather x1 -> x0, waiting for transfers between devices: 59.9 us -> none  [local(): lax.all_gather(w_inner, ('batch', 'ctx'), axis=0, tiled=True)]
    all_gather x1, waiting for transfers between devices: 22.7 us -> 53 us  [local(): lax.all_gather(key_flat, 'ctx', axis=0, tiled=True)]
  transfers between devices with their start and end apart: 9 -> 9, of which waited for: 7 -> 6; matrix products, arithmetic and copies ran while one was open for 8% -> 9% of each run, Pallas kernels for 0% -> 0%
where the time goes in v1:
time: 619 us; the launch traced here: 618 us
  waiting for transfers between devices  411 us (66%)
  blocking collectives  72.8 us (12%)
  matrix products  61.7 us (10%)
  local copies, waits for them, and re-layouts  44.7 us (7%)
  between operations  14.7 us (2%)
  other arithmetic  8.55 us (1%)
    reduce_scatter x1, waiting for transfers between devices, local(): lax.psum_scatter(grad_rows(jnp.int32(0), owned_rows * lax.axis_size(('bat...  210 us
    all_gather x1, waiting for transfers between devices, local(): lax.all_gather(key_flat, 'ctx', axis=0, tiled=True)  53 us
    all_gather x1, waiting for transfers between devices, local(): lax.all_gather(w_down, ('batch', 'ctx'), axis=0, tiled=True)  52.6 us
    all_gather x1, waiting for transfers between devices, local(): lax.all_gather(w_proj, ('batch', 'ctx'), axis=0, tiled=True)  48.5 us
    unnamed x1, blocking collectives  42.2 us
    all_gather x1, waiting for transfers between devices, local(): lax.all_gather(value_flat, 'ctx', axis=0, tiled=True)  25.6 us
    concatenate x1, local copies, waits for them, and re-layouts, grad_rows(): jnp.concatenate([jnp.einsum('td,te->de', h_one, d_projected, preferred_el...  22.2 us
    all_gather x1, waiting for transfers between devices, local(): lax.all_gather(w_qkv, ('batch', 'ctx'), axis=0, tiled=True)  19.8 us
  transfers between devices with their start and end apart: 9, of which 6 were waited for; matrix products, arithmetic and copies ran while one was open for 9% of the time, Pallas kernels for 0%

profile of v1, /device:TPU:0, one launch (start us, length us, event | category | flops | bytes accessed | tf_op | source)
XLA Modules:
  0.0 617.6 jit_solution(5800443226296703146)
XLA Ops:
  8.0 0.8 dynamic-update-slice
  8.8 0.8 dynamic-update-slice.1
  9.7 42.2 %all-reduce.2 = (bf16[768]{0:T(1024)(128)(2,1)S(1)}, bf16[768]{0:T(1024)(128)(2,1)S(1)}) all-reduce(bf16[768]{0:T(1024)(128)(2,1)S(1)} %dynamic-update-slice, bf16[768]{0:T(1024)(128)(2,1)S(1)} %dynamic-update-slice.1), channel_id=1, replica_groups=mesh['batch'=4,'ctx'=8] {'batch','ctx'}, use_global_device_ids=true, to_apply=%add | all-reduce | flops 1536 | bytes 6144
  51.9 1.0 convert_reduce_fusion
  53.0 1.1 fusion.58
  54.1 19.8 %all-gather.8.cloned.1.call-done = bf16[768,2304]{1,0:T(8,128)(2,1)} async-done(((bf16[24,2304]{1,0:T(8,128)(2,1)}), bf16[768,2304]{1,0:T(8,128)(2,1)}) %all-gather.8.cloned.1.call-update) | async-done | bytes 3538960 | tf_op jit(solution)/shard_map/all_gather | solution.py:95
  73.9 2.8 fusion.79
  80.7 2.0 tile.2
  82.7 3.6 all-to-all-start
  87.7 25.6 %all-gather.12.cloned.1.call-done = bf16[1024,768]{1,0:T(8,128)(2,1)} async-done(((bf16[128,768]{1,0:T(8,128)(2,1)}), bf16[1024,768]{1,0:T(8,128)(2,1)}) %all-gather.12.cloned.1.call-update) | async-done | bytes 1572880 | tf_op jit(solution)/shard_map/all_gather | solution.py:123
  113.3 1.7 copy.27
  115.0 53.0 %all-gather.10.cloned.1.call-done = bf16[1024,768]{0,1:T(8,128)(2,1)} async-done(((bf16[128,768]{0,1:T(8,128)(2,1)}), bf16[1024,768]{0,1:T(8,128)(2,1)}) %all-gather.10.cloned.1.call-update) | async-done | bytes 1572880 | tf_op jit(solution)/shard_map/all_gather | solution.py:122
  168.0 2.5 multiply_reduce_fusion
  170.5 1.3 fusion
  171.9 1.3 copy-done
  173.2 1.5 fusion.35
  174.6 48.5 %all-gather.14.cloned.1.call-done = bf16[768,768]{1,0:T(8,128)(2,1)} async-done(((bf16[24,768]{1,0:T(8,128)(2,1)}), bf16[768,768]{1,0:T(8,128)(2,1)}) %all-gather.14.cloned.1.call-update) | async-done | bytes 1179664 | tf_op jit(solution)/shard_map/all_gather | solution.py:96
  223.2 1.7 fusion.84
  225.1 2.7 fusion.81
  227.8 52.6 %all-gather.16.cloned.1.call-done = bf16[768,1152]{1,0:T(8,128)(2,1)} async-done(((bf16[24,1152]{1,0:T(8,128)(2,1)}), bf16[768,1152]{1,0:T(8,128)(2,1)}) %all-gather.16.cloned.1.call-update) | async-done | bytes 1769488 | tf_op jit(solution)/shard_map/all_gather | solution.py:98
  280.4 2.1 fusion.43
  282.5 3.6 multiply_reduce_fusion.1
  286.4 1.2 convolution_convert_fusion
  287.7 0.8 copy.30
  288.5 1.1 copy.28
  289.6 0.9 broadcast_in_dim.19
  290.5 15.3 %all_gather.43 = f32[12,1024]{1,0:T(8,128)} all-gather(f32[12,128]{1,0:T(8,128)S(1)} %get-tuple-element.36), channel_id=1, replica_groups=mesh['batch'=4,'ctx'=8] {'ctx'}, dimensions={1}, use_global_device_ids=true | all-gather | bytes 55296 | tf_op jit(solution)/shard_map/all_gather | solution.py:186
  305.9 15.2 %all_gather.45 = f32[12,1024]{1,0:T(8,128)} all-gather(f32[12,128]{1,0:T(8,128)S(1)} %bitcast.129), channel_id=1, replica_groups=mesh['batch'=4,'ctx'=8] {'ctx'}, dimensions={1}, use_global_device_ids=true | all-gather | bytes 55296 | tf_op jit(solution)/shard_map/all_gather | solution.py:187
  321.6 3.8 convolution_bitcast_fusion
  325.4 4.1 fusion.59
  329.6 5.1 fusion.85
  334.7 7.3 %fusion.23 = f32[128,12,64]{0,2,1:T(8,128)} fusion(bf16[1024,12,64]{0,2,1:T(8,128)(2,1)} %bitcast.115, f32[12,128,1024]{2,1,0:T(8,128)} %copy-done, f32[12,128]{1,0:T(8,128)S(1)} %bitcast.130, f32[12,128]{1,0:T(8,128)} %copy-done.21, bf16[128,12,64]{0,2,1:T(8,128)(2,1)} %bitcast.121, bf16[1024,12,64]{0,2,1:T(8,128)(2,1)} %bitcast.111), kind=kOutput, calls=%fused_computation.25 | convolution fusion | flops 410615808 | bytes 10039296 | tf_op jit(solution)/shard_map/hqk,khd->qhd/dot_general | solution.py:199
  341.9 2.6 copy.29
  344.5 4.5 fusion.28
  349.0 8.9 %fusion.21 = f32[128,12,64]{0,2,1:T(8,128)} fusion(bf16[1024,12,64]{0,2,1:T(8,128)(2,1)} %bitcast.117, f32[12,1024,128]{2,1,0:T(8,128)} %fusion.85, f32[12,1024]{1,0:T(8,128)} %all_gather.45, f32[12,1024]{1,0:T(8,128)} %all_gather.43, bf16[1024,12,64]{0,2,1:T(8,128)(2,1)} %bitcast.107, bf16[128,12,64]{0,2,1:T(8,128)(2,1)} %bitcast.128), kind=kOutput, calls=%fused_computation.23 | convolution fusion | flops 410615808 | bytes 10125312 | tf_op jit(solution)/shard_map/hqk,qhd->khd/dot_general | solution.py:212
  357.9 1.4 subtract_convert_fusion.1
  359.3 4.1 fusion.61
  363.4 2.6 fusion.57
  366.0 0.9 broadcast_in_dim.18
  367.0 22.2 %concatenate.31 = f32[768,6530]{1,0:T(8,128)} concatenate(f32[768,2304]{1,0:T(8,128)} %fusion.61, f32[768,768]{1,0:T(8,128)S(1)} %fusion.66, f32[768,2304]{1,0:T(8,128)} %fusion.59, f32[768,1152]{1,0:T(8,128)} %convolution_bitcast_fusion, f32[768,1]{1,0:T(8,128)} %broadcast_in_dim.18, f32[768,1]{1,0:T(8,128)} %broadcast_in_dim.19), dimensions={1} | concatenate | bytes 40120320 | tf_op jit(solution)/shard_map/concatenate | solution.py:235
  389.2 1.2 copy-done.4
  390.5 2.9 fusion.31
  393.4 0.9 fusion.56
  394.3 210.1 %reduce-scatter.2.cloned.1.call-done = f32[24,6530]{1,0:T(8,128)} async-done(((f32[768,6530]{1,0:T(8,128)}), f32[24,6530]{1,0:T(8,128)}) %reduce-scatter.2.cloned.1.call-update) | async-done | bytes 626896 | tf_op jit(solution)/shard_map/reduce_scatter | solution.py:248
  604.4 1.5 slice_reduce_fusion
  605.9 1.5 slice.91
  607.4 1.5 slice.93
  608.9 1.8 fusion.83
  (108 shorter events, 7.2 us)
Async XLA Ops:
  7.2 66.7 %all-gather.8.cloned.1.call-start = ((), (), s32[]{:S(2)}) async-start(), calls=%async_computation.2 | async-start | bytes 3649536 | tf_op jit(solution)/shard_map/all_gather | solution.py:95
  7.9 105.4 %all-gather.12.cloned.1.call-start = ((), (), s32[]{:S(2)}) async-start(), calls=%async_computation.4 | async-start | bytes 1769472 | tf_op jit(solution)/shard_map/all_gather | solution.py:123
  52.9 24.6 %copy-start.22 = (f32[128]{0:T(128)}, f32[128]{0:T(128)S(1)}, u32[]{:S(2)}) copy-start(f32[128]{0:T(128)S(1)} %broadcast_multiply_fusion.6) | copy-start | bytes 1540
  54.1 23.4 %copy-start.26 = (f32[128]{0:T(128)}, f32[128]{0:T(128)S(1)}, u32[]{:S(2)}) copy-start(f32[128]{0:T(128)S(1)} %add_rsqrt_fusion.1) | copy-start | bytes 1540
  76.7 4.0 copy-start.20
  77.4 90.6 %all-gather.10.cloned.1.call-start = ((), (), s32[]{:S(2)}) async-start(), calls=%async_computation.3 | async-start | bytes 1769472 | tf_op jit(solution)/shard_map/all_gather | solution.py:122
  78.3 4.4 copy-start.19
  78.8 0.6 copy-start.8
  78.8 1.3 copy-start.10
  80.1 143.0 %all-gather.14.cloned.1.call-start = ((), (), s32[]{:S(2)}) async-start(), calls=%async_computation.5 | async-start | bytes 1216512 | tf_op jit(solution)/shard_map/all_gather | solution.py:96
  82.7 142.4 %all-to-all-start = ((bf16[32,24,2304]{2,1,0:T(8,128)(2,1)}), bf16[32,24,2304]{2,1,0:T(8,128)(2,1)}, u32[]{:S(2)}, u32[]{:S(2)}) async-start(bf16[32,24,2304]{2,1,0:T(8,128)(2,1)} %tile.2), calls=%async_computation | async-start | bytes 7077888 | tf_op jit(solution)/shard_map/all_to_all | solution.py:87
  86.3 194.1 %all-gather.16.cloned.1.call-start = ((), (), s32[]{:S(2)}) async-start(), calls=%async_computation.6 | async-start | bytes 1824768 | tf_op jit(solution)/shard_map/all_gather | solution.py:98
  86.9 242.7 %all-gather.18.cloned.1.call-start = ((), (), s32[]{:S(2)}) async-start(), calls=%async_computation.7 | async-start | bytes 1769472 | tf_op jit(solution)/shard_map/all_gather | solution.py:203
  87.6 254.3 %all-gather.20.cloned.1.call-start = ((), (), s32[]{:S(2)}) async-start(), calls=%async_computation.8 | async-start | bytes 1769472 | tf_op jit(solution)/shard_map/all_gather | solution.py:204
  115.0 56.8 %copy-start.7 = (bf16[1024,768]{0,1:T(8,128)(2,1)}, bf16[1024,768]{0,1:T(8,128)(2,1)S(1)}, u32[]{:S(2)}) copy-start(bf16[1024,768]{0,1:T(8,128)(2,1)S(1)} %copy.27) | copy-start | bytes 4718596
  170.5 2.7 copy-start
  171.8 118.7 %copy-start.21 = (f32[12,128]{1,0:T(8,128)}, f32[12,128]{1,0:T(8,128)S(1)}, u32[]{:S(2)}) copy-start(f32[12,128]{1,0:T(8,128)S(1)} %get-tuple-element.36) | copy-start | bytes 18436
  173.2 50.0 %copy-start.1 = (bf16[1,128,768]{2,1,0:T(8,128)(2,1)S(1)}, bf16[1,128,768]{2,1,0:T(8,128)(2,1)}, u32[]{:S(2)}) copy-start(bf16[1,128,768]{2,1,0:T(8,128)(2,1)} %param.8) | copy-start | bytes 589828
  224.9 55.5 %copy-start.12 = (bf16[1,128,768]{2,1,0:T(8,128)(2,1)S(1)}, bf16[1,128,768]{2,1,0:T(8,128)(2,1)}, u32[]{:S(2)}) copy-start(bf16[1,128,768]{2,1,0:T(8,128)(2,1)} %param.9) | copy-start | bytes 589828
  224.9 61.3 %copy-start.24 = (f32[128]{0:T(128)}, f32[128]{0:T(128)S(1)}, u32[]{:S(2)}) copy-start(f32[128]{0:T(128)S(1)} %broadcast_multiply_fusion.5) | copy-start | bytes 1540
  225.1 61.1 %copy-start.28 = (f32[128]{0:T(128)}, f32[128]{0:T(128)S(1)}, u32[]{:S(2)}) copy-start(f32[128]{0:T(128)S(1)} %add_rsqrt_fusion) | copy-start | bytes 1540
  227.8 54.7 %copy-start.3 = (f32[128,2304]{1,0:T(8,128)}, f32[128,2304]{1,0:T(8,128)S(1)}, u32[]{:S(2)}) copy-start(f32[128,2304]{1,0:T(8,128)S(1)} %fusion.81) | copy-start | bytes 3538948
  282.5 3.7 copy-start.17
  282.5 3.9 copy-start.15
  282.5 3.9 copy-start.2
  282.5 5.2 copy-start.6
  287.6 316.7 %reduce-scatter.2.cloned.1.call-start = ((), (), s32[]{:S(2)}) async-start(), calls=%async_computation.9 | async-start | bytes 21086208 | tf_op jit(solution)/shard_map/reduce_scatter | solution.py:248
  289.6 16.3 %copy-start.13 = (bf16[128,768]{0,1:T(8,128)(2,1)}, bf16[128,768]{0,1:T(8,128)(2,1)S(1)}, u32[]{:S(2)}) copy-start(bf16[128,768]{0,1:T(8,128)(2,1)S(1)} %copy.28) | copy-start | bytes 589828
  321.1 4.2 copy-start.16
  321.1 4.2 copy-start.18
  321.1 4.2 copy-start.25
  321.1 4.2 copy-start.29
  325.4 4.2 copy-start.9
  325.4 4.2 copy-start.11
  349.0 10.3 %copy-start.23 = (f32[128]{0:T(128)S(1)}, f32[128]{0:T(128)}, u32[]{:S(2)}) copy-start(f32[128]{0:T(128)} %copy-done.22) | copy-start | bytes 1540
  349.0 10.3 %copy-start.27 = (f32[128]{0:T(128)S(1)}, f32[128]{0:T(128)}, u32[]{:S(2)}) copy-start(f32[128]{0:T(128)} %copy-done.26) | copy-start | bytes 1540
  359.3 4.1 copy-start.5
  389.2 1.3 copy-start.4
  389.2 4.2 copy-start.30
  390.5 2.9 copy-start.14
Sparse Core Ops, SparseCore 0:
  11.0 62.8 all-gather.7
  77.5 35.7 all-gather.11
  115.5 52.4 all-gather.9
  170.9 52.2 all-gather.13
  225.9 54.4 all-gather.15
  282.4 26.3 all-gather.17
  311.1 25.7 all-gather.19
  389.3 215.0 reduce-scatter.1
